TPU v7x, 32 devices: a whole 2x2x4 slice. The times are simulated.
32 devices in a mesh: seq: 8 (over z, y), head: 4 (over x, core).
Axes of the slice: x: 2, y: 2, z: 4, core: 2. Of those that a mesh axis runs over, the one named last changes fastest.
Arguments:
- inputs: bfloat16 [4, 4096, 768], P(None, 'seq'), may hold values from -6 to 6
- w_qkv: bfloat16 [3, 768, 768], P(None, None, 'head'), may hold values from -0.21875 to 0.21875
- b_qv: bfloat16 [2, 768], P(None, 'head'), may hold values from -4 to 4
- w_out: bfloat16 [768, 768], P('head'), may hold values from -1 to 1
- out_bias: bfloat16 [2, 768], replicated, may hold values from -4 to 4
- w_up: bfloat16 [768, 3072], P(None, 'head'), may hold values from -0.21875 to 0.21875
- b_up: bfloat16 [3072], P('head'), may hold values from -4 to 4
- w_down: bfloat16 [3072, 768], P('head'), may hold values from -0.109375 to 0.109375
- norm_gain: float32 [2, 768], replicated, may hold values from 0.5 to 1.5
- norm_shift: float32 [2, 768], replicated, may hold values from -3 to 3
- d_out: bfloat16 [4, 4096, 768], P(None, ('seq', 'head')), may hold values from -6 to 6
- q_perm: int32 [4, 12, 4096], P(None, 'head'), may hold values from 0 to 4095, as said below
- k_perm: int32 [4, 12, 4096], P(None, 'head'), may hold values from 0 to 4095, as said below
- masked: int32 [4, 1024], replicated, may hold values from 0 to 4095, as said below
Outputs:
- result: float32 [4, 4096, 768], P(None, ('seq', 'head'))
- d_inputs: float32 [4, 4096, 768], P(None, ('seq', 'head'))
- grad_qkv: float32 [3, 768, 768], P(None, 'seq', 'head')
- grad_bqv: float32 [2, 768], replicated
- grad_wout: float32 [768, 768], P('head', 'seq')
- grad_obias: float32 [2, 768], replicated
- grad_wup: float32 [768, 3072], P('seq', 'head')
- grad_bup: float32 [3072], replicated
- grad_wdown: float32 [3072, 768], P('head', 'seq')
- grad_gain: float32 [2, 768], replicated
- grad_shift: float32 [2, 768], replicated
- entropy: float32 [12, 128], P('head', 'seq')
- occupancy: int32 [12, 128], P('head', 'seq')
Inputs may be any that keep to these rules, and one draw needn't show every extreme that they name: `q_perm`: for each sequence and head a permutation of the 4096 positions. Cut the positions into aligned blocks of 512 and the slots into aligned runs of 2048: one block puts between 171 and 341 of its positions into one run, and 341 is reached for every sequence and head. `k_perm`: same law as q_perm, drawn independently. `masked`: each row lists 1024 distinct positions in increasing order.
All inputs are finite; a program needn't handle non-finite values.
Results may differ from a plain program's by a relative error of at most 0.015.
Values may be sent and summed in bfloat16 or wider, within the bound.
No kernel may reach another device: no remote copies, remote signals or barrier semaphores. Data moves between devices by JAX's collectives and lax.ppermute only.
A program may use at most 192 MiB of HBM per device.

v0:
```python
import math

import jax
import jax.numpy as jnp
from jax import lax
from jax.sharding import PartitionSpec as P

DH = 64
FF = 3072
CLUSTER = 128
LENGTH = 4096
TOK_DEV = 2048


EPS = 1e-06


def split_up(x, dim, length):
    before, after = (x.shape[:dim], x.shape[dim + 1 :])
    return jnp.moveaxis(x.reshape(*before, length, -1, *after), dim, 0)


def sum_at_owner(x, axis, dim):
    length = lax.axis_size(axis)
    tiles = lax.all_to_all(split_up(x, dim, length), axis, 0, 0, tiled=True)
    return jnp.sum(tiles.astype(jnp.float32), axis=0)


def layer_norm(values, gain_row, shift_row):
    row_mean = jnp.mean(values, -1, keepdims=True)
    centred = values - row_mean
    variance = jnp.mean(centred * centred, -1, keepdims=True)
    inv_std = lax.rsqrt(variance + EPS)
    normed = centred * inv_std
    return (normed * gain_row + shift_row, normed, inv_std)


def norm_back(grad_in, normed, inv_std, gain_row):
    scaled = grad_in * gain_row
    inner_term = (
        scaled
        - jnp.mean(scaled, -1, keepdims=True)
        - normed * jnp.mean(scaled * normed, -1, keepdims=True)
    )
    return inner_term * inv_std


def before_matrix(count):
    slot_ids = jnp.arange(count, dtype=jnp.int32)
    return (slot_ids[:, None] < slot_ids[None, :]).astype(jnp.bfloat16)


def sender_select(slot_order, block_start, block_len, capacity, earlier):
    seq_count, heads, length = slot_order.shape
    owners = length // TOK_DEV
    runs = slot_order.reshape(seq_count, heads, owners, TOK_DEV).transpose(0, 2, 1, 3)
    group_size = math.gcd(seq_count, 4)
    grouped = runs.reshape(seq_count // group_size, group_size, owners, heads, TOK_DEV)
    rank_levels = jnp.arange(capacity, dtype=jnp.int32)
    pos_levels = jnp.arange(block_len, dtype=jnp.int32)

    def one_group(group):
        local = group - block_start
        inside = (local >= 0) & (local < block_len)
        ranks = jnp.einsum(
            "gohi,ij->gohj",
            inside.astype(jnp.bfloat16),
            earlier,
            preferred_element_type=jnp.float32,
        ).astype(jnp.int32)
        rank_hot = ((ranks[..., None] == rank_levels) & inside[..., None]).astype(jnp.bfloat16)
        pos_hot = (local[..., None] == pos_levels).astype(jnp.bfloat16)
        return jnp.einsum(
            "gohjr,gohjp->gohrp", rank_hot, pos_hot, preferred_element_type=jnp.float32
        ).astype(jnp.bfloat16)

    selected = lax.map(one_group, grouped)
    return selected.reshape(seq_count, owners, heads, capacity, block_len)


def receiver_hot(slot_order, seq_owned, owner_part, block_len, seq_devices, capacity, earlier):
    seq_order = lax.dynamic_index_in_dim(slot_order, seq_owned, 0, keepdims=False)
    positions = lax.dynamic_slice_in_dim(seq_order, owner_part * TOK_DEV, TOK_DEV, 1)
    sources = positions // block_len
    source_hot = (sources[..., None] == jnp.arange(seq_devices, dtype=jnp.int32)).astype(
        jnp.bfloat16
    )
    counted = jnp.einsum("hin,ij->hjn", source_hot, earlier, preferred_element_type=jnp.float32)
    ranks = jnp.sum(counted * source_hot.astype(jnp.float32), -1).astype(jnp.int32)
    columns = sources * capacity + ranks
    hot = (columns[..., None] == jnp.arange(seq_devices * capacity, dtype=jnp.int32)).astype(
        jnp.bfloat16
    )
    return (positions, hot)


def pack_rows(row_data, selected):
    packed = jnp.einsum(
        "sohrp,sphx->sohrx", selected, row_data, preferred_element_type=jnp.float32
    ).astype(jnp.bfloat16)
    return packed.reshape(
        packed.shape[0] * packed.shape[1], packed.shape[2], packed.shape[3], packed.shape[4]
    )


def unpack_rows(buffer, selected):
    seq_count, owners = (selected.shape[0], selected.shape[1])
    shaped = buffer.reshape(seq_count, owners, buffer.shape[1], buffer.shape[2], buffer.shape[3])
    return jnp.einsum(
        "sohrp,sohrx->sphx", selected, shaped, preferred_element_type=jnp.float32
    ).astype(jnp.bfloat16)


def place_rows(row_data, hot, seq_devices, capacity):
    placed = jnp.einsum("hjc,hjx->hcx", hot, row_data, preferred_element_type=jnp.float32).astype(
        jnp.bfloat16
    )
    placed = placed.reshape(row_data.shape[0], seq_devices, capacity, row_data.shape[2])
    return jnp.transpose(placed, (1, 0, 2, 3))


def take_rows(buffer, hot):
    heads = buffer.shape[1]
    flat = jnp.transpose(buffer, (1, 0, 2, 3)).reshape(
        heads, buffer.shape[0] * buffer.shape[2], buffer.shape[3]
    )
    return jnp.einsum("hjc,hcx->hjx", hot, flat, preferred_element_type=jnp.float32).astype(
        jnp.bfloat16
    )


def per_device(
    inputs,
    w_qkv,
    b_qv,
    w_out,
    out_bias,
    w_up,
    b_up,
    w_down,
    norm_gain,
    norm_shift,
    d_out,
    q_perm,
    k_perm,
    masked,
):
    seq_devices = lax.axis_size("seq")
    head_devices = lax.axis_size("head")
    seq_index = lax.axis_index("seq")
    head_index = lax.axis_index("head")
    seq_count, block_len, model_width = inputs.shape
    local_heads = q_perm.shape[1]
    head_cols = local_heads * DH
    owner_count = LENGTH // TOK_DEV
    mean_rows = block_len // owner_count
    capacity = mean_rows + mean_rows // 3
    share_rows = block_len // head_devices
    group_count = TOK_DEV // CLUSTER
    score_scale = DH ** (-0.5)
    seq_owned = seq_index // owner_count
    owner_part = seq_index % owner_count
    token_count = seq_count * block_len
    earlier = before_matrix(TOK_DEV)
    tokens_flat = inputs.reshape(token_count, model_width)
    projected = jnp.einsum("td,kdc->ktc", tokens_flat, w_qkv, preferred_element_type=jnp.float32)
    bias_qv = b_qv.astype(jnp.float32)
    queries = (
        (projected[0] + bias_qv[0])
        .astype(jnp.bfloat16)
        .reshape(seq_count, block_len, local_heads, DH)
    )
    keys_local = projected[1].astype(jnp.bfloat16).reshape(seq_count, block_len, local_heads, DH)
    values_local = (
        (projected[2] + bias_qv[1])
        .astype(jnp.bfloat16)
        .reshape(seq_count, block_len, local_heads, DH)
    )
    key_value = jnp.concatenate([keys_local, values_local], -1)
    q_select = sender_select(q_perm, seq_index * block_len, block_len, capacity, earlier)
    k_select = sender_select(k_perm, seq_index * block_len, block_len, capacity, earlier)
    q_send = pack_rows(queries, q_select)
    kv_send = pack_rows(key_value, k_select)
    q_recv, kv_recv = (
        lax.all_to_all(q_send, "seq", split_axis=0, concat_axis=0, tiled=True),
        lax.all_to_all(kv_send, "seq", split_axis=0, concat_axis=0, tiled=True),
    )
    q_positions, q_hot = receiver_hot(
        q_perm, seq_owned, owner_part, block_len, seq_devices, capacity, earlier
    )
    k_hot = receiver_hot(k_perm, seq_owned, owner_part, block_len, seq_devices, capacity, earlier)[
        1
    ]
    q_cluster = take_rows(q_recv, q_hot).reshape(local_heads, group_count, CLUSTER, DH)
    kv_cluster = take_rows(kv_recv, k_hot).reshape(local_heads, group_count, CLUSTER, 2 * DH)
    k_cluster = kv_cluster[..., :DH]
    v_cluster = kv_cluster[..., DH:]
    scores = (
        jnp.einsum("hgqe,hgke->hgqk", q_cluster, k_cluster, preferred_element_type=jnp.float32)
        * score_scale
    )
    log_total = jax.nn.logsumexp(scores, -1)
    soft_weights = jnp.exp(scores - log_total[..., None])
    entropy = jnp.mean(log_total - jnp.sum(soft_weights * scores, -1), -1)
    attended = jnp.einsum(
        "hgqk,hgke->hgqe",
        soft_weights.astype(jnp.bfloat16),
        v_cluster,
        preferred_element_type=jnp.float32,
    )
    attended = attended.astype(jnp.bfloat16).reshape(local_heads, TOK_DEV, DH)
    back_recv = lax.all_to_all(
        place_rows(attended, q_hot, seq_devices, capacity),
        "seq",
        split_axis=0,
        concat_axis=0,
        tiled=True,
    )
    head_rows = unpack_rows(back_recv, q_select).reshape(token_count, head_cols)
    attn_part = jnp.dot(head_rows, w_out, preferred_element_type=jnp.float32).reshape(
        seq_count, block_len, model_width
    )
    bias_out = out_bias.astype(jnp.float32)
    attn_whole = lax.psum(attn_part, "head")
    first_all, normed_all, inv_all = layer_norm(
        inputs.astype(jnp.float32) + attn_whole + bias_out[0], norm_gain[0], norm_shift[0]
    )
    first_low = first_all.astype(jnp.bfloat16)
    first_out = lax.dynamic_slice_in_dim(first_all, head_index * share_rows, share_rows, 1)
    normed_one = lax.dynamic_slice_in_dim(normed_all, head_index * share_rows, share_rows, 1)
    inv_one = lax.dynamic_slice_in_dim(inv_all, head_index * share_rows, share_rows, 1)
    low_flat = first_low.reshape(token_count, model_width)
    upper_in = jnp.dot(low_flat, w_up, preferred_element_type=jnp.float32) + b_up.astype(
        jnp.float32
    )
    gelu_out, gelu_back = jax.vjp(
        lambda upper_val: jax.nn.gelu(upper_val, approximate=False), upper_in
    )
    hidden_low = gelu_out.astype(jnp.bfloat16)
    ffn_part = jnp.dot(hidden_low, w_down, preferred_element_type=jnp.float32).reshape(
        seq_count, block_len, model_width
    )
    ffn_share = lax.psum_scatter(ffn_part, "head", scatter_dimension=1, tiled=True)
    result, normed_two, inv_two = layer_norm(
        first_out + ffn_share + bias_out[1], norm_gain[1], norm_shift[1]
    )
    share_start = seq_index * block_len + head_index * share_rows
    share_positions = share_start + jnp.arange(share_rows, dtype=jnp.int32)
    mask_share = jnp.any(masked[:, :, None] == share_positions[None, None, :], 1).astype(
        jnp.float32
    )
    seed_grad = d_out.astype(jnp.float32) * mask_share[..., None]
    gain_two = jnp.sum(seed_grad * normed_two, (0, 1))
    shift_two = jnp.sum(seed_grad, (0, 1))
    d_second = norm_back(seed_grad, normed_two, inv_two, norm_gain[1])
    bias_ffn_grad = jnp.sum(d_second, (0, 1))
    d_rows = lax.all_gather(d_second.astype(jnp.bfloat16), "head", axis=1, tiled=True)
    d_flat = d_rows.reshape(token_count, model_width)
    grad_down = jnp.einsum("tf,td->fd", hidden_low, d_flat, preferred_element_type=jnp.float32)
    d_hidden = jnp.einsum("td,fd->tf", d_flat, w_down, preferred_element_type=jnp.float32)
    d_upper = gelu_back(d_hidden)[0]
    grad_bup = jnp.sum(d_upper, 0)
    d_upper_low = d_upper.astype(jnp.bfloat16)
    grad_up = jnp.einsum("td,tf->df", low_flat, d_upper_low, preferred_element_type=jnp.float32)
    d_first_part = jnp.einsum(
        "tf,df->td", d_upper_low, w_up, preferred_element_type=jnp.float32
    ).reshape(seq_count, block_len, model_width)
    d_first = d_second + lax.psum_scatter(
        d_first_part.astype(jnp.bfloat16), "head", scatter_dimension=1, tiled=True
    ).astype(jnp.float32)
    gain_one = jnp.sum(d_first * normed_one, (0, 1))
    shift_one = jnp.sum(d_first, (0, 1))
    d_first_in = norm_back(d_first, normed_one, inv_one, norm_gain[0])
    bias_attn_grad = jnp.sum(d_first_in, (0, 1))
    d_attn = lax.all_gather(d_first_in.astype(jnp.bfloat16), "head", axis=1, tiled=True)
    d_attn_flat = d_attn.reshape(token_count, model_width)
    grad_wout = jnp.einsum("tc,td->cd", head_rows, d_attn_flat, preferred_element_type=jnp.float32)
    d_heads = jnp.einsum("td,cd->tc", d_attn_flat, w_out, preferred_element_type=jnp.float32)
    d_heads = d_heads.astype(jnp.bfloat16).reshape(seq_count, block_len, local_heads, DH)
    d_recv = lax.all_to_all(
        pack_rows(d_heads, q_select), "seq", split_axis=0, concat_axis=0, tiled=True
    )
    d_cluster = take_rows(d_recv, q_hot).reshape(local_heads, group_count, CLUSTER, DH)
    scores_again = (
        jnp.einsum("hgqe,hgke->hgqk", q_cluster, k_cluster, preferred_element_type=jnp.float32)
        * score_scale
    )
    soft_again = jnp.exp(scores_again - log_total[..., None])
    grad_value = jnp.einsum(
        "hgqk,hgqe->hgke",
        soft_again.astype(jnp.bfloat16),
        d_cluster,
        preferred_element_type=jnp.float32,
    )
    d_soft = jnp.einsum("hgqe,hgke->hgqk", d_cluster, v_cluster, preferred_element_type=jnp.float32)
    d_scores = soft_again * (d_soft - jnp.sum(soft_again * d_soft, -1, keepdims=True))
    d_raw = (d_scores * score_scale).astype(jnp.bfloat16)
    grad_query = jnp.einsum("hgqk,hgke->hgqe", d_raw, k_cluster, preferred_element_type=jnp.float32)
    grad_query = grad_query.astype(jnp.bfloat16).reshape(local_heads, TOK_DEV, DH)
    grad_key = jnp.einsum(
        "hgqk,hgqe->hgke", d_raw, q_cluster, preferred_element_type=jnp.float32
    ).astype(jnp.bfloat16)
    grad_kv = jnp.concatenate([grad_key, grad_value.astype(jnp.bfloat16)], -1).reshape(
        local_heads, TOK_DEV, 2 * DH
    )
    gq_send = place_rows(grad_query, q_hot, seq_devices, capacity)
    gkv_send = place_rows(grad_kv, k_hot, seq_devices, capacity)
    gq_recv, gkv_recv = (
        lax.all_to_all(gq_send, "seq", split_axis=0, concat_axis=0, tiled=True),
        lax.all_to_all(gkv_send, "seq", split_axis=0, concat_axis=0, tiled=True),
    )
    d_query = unpack_rows(gq_recv, q_select).reshape(token_count, head_cols)
    d_kv_rows = unpack_rows(gkv_recv, k_select)
    d_key = d_kv_rows[..., :DH].reshape(token_count, head_cols)
    d_value = d_kv_rows[..., DH:].reshape(token_count, head_cols)
    d_stack = jnp.stack([d_query, d_key, d_value])
    grad_qkv = jnp.einsum("td,ktc->kdc", tokens_flat, d_stack, preferred_element_type=jnp.float32)
    d_in_part = jnp.einsum(
        "ktc,kdc->td", d_stack, w_qkv, preferred_element_type=jnp.float32
    ).reshape(seq_count, block_len, model_width)
    d_inputs = d_first_in + lax.psum_scatter(
        d_in_part.astype(jnp.bfloat16), "head", scatter_dimension=1, tiled=True
    ).astype(jnp.float32)
    grad_bq = jnp.sum(d_query.astype(jnp.float32), 0)
    grad_bv = jnp.sum(d_value.astype(jnp.float32), 0)
    qkv_sum, wout_sum, up_sum, down_sum = (
        sum_at_owner(grad_qkv.astype(jnp.bfloat16), "seq", 1),
        sum_at_owner(grad_wout.astype(jnp.bfloat16), "seq", 1),
        sum_at_owner(grad_up.astype(jnp.bfloat16), "seq", 0),
        sum_at_owner(grad_down.astype(jnp.bfloat16), "seq", 1),
    )
    bqv_full = lax.dynamic_update_slice_in_dim(
        jnp.zeros((2, model_width), jnp.float32),
        jnp.stack([grad_bq, grad_bv]),
        head_index * head_cols,
        1,
    )
    bup_full = lax.dynamic_update_slice_in_dim(
        jnp.zeros((FF,), jnp.float32), grad_bup, head_index * grad_bup.shape[0], 0
    )
    bqv_sum, obias_sum, bup_sum, gain_sum, shift_sum = lax.psum(
        (
            bqv_full,
            jnp.stack([bias_attn_grad, bias_ffn_grad]),
            bup_full,
            jnp.stack([gain_one, gain_two]),
            jnp.stack([shift_one, shift_two]),
        ),
        ("seq", "head"),
    )
    masked_row = lax.dynamic_index_in_dim(masked, seq_owned, 0, keepdims=False)
    slot_masked = jnp.any(q_positions[..., None] == masked_row[None, None, :], -1).astype(jnp.int32)
    occupancy = jnp.sum(slot_masked.reshape(local_heads, group_count, CLUSTER), -1)
    return (
        result,
        d_inputs,
        qkv_sum,
        bqv_sum,
        wout_sum,
        obias_sum,
        up_sum,
        bup_sum,
        down_sum,
        gain_sum,
        shift_sum,
        entropy,
        occupancy,
    )


def solution(mesh):
    placed = (
        P(None, "seq", None),
        P(None, None, "head"),
        P(None, "head"),
        P("head", None),
        P(),
        P(None, "head"),
        P("head"),
        P("head", None),
        P(),
        P(),
        P(None, ("seq", "head"), None),
        P(None, "head", None),
        P(None, "head", None),
        P(),
    )
    return jax.shard_map(
        per_device,
        mesh=mesh,
        in_specs=placed,
        out_specs=(
            P(None, ("seq", "head"), None),
            P(None, ("seq", "head"), None),
            P(None, "seq", "head"),
            P(),
            P("head", "seq"),
            P(),
            P("seq", "head"),
            P(),
            P("head", "seq"),
            P(),
            P(),
            P("head", "seq"),
            P("head", "seq"),
        ),
        check_vma=False,
    )
```

profile of v0, /device:TPU:0, one launch (start us, length us, event | category | flops | bytes accessed | tf_op | source)
XLA Modules:
  0.0 967.4 jit_solution(402779239757419517)
XLA Ops:
  19.3 11.6 %fusion.251 = pred[4,2,3,2048,341]{3,4,2,1,0:T(8,128)(4,1)S(1)} fusion(s32[4,2,3,2048]{3,2,1,0:T(4,128)S(1)} %fusion.72, pred[4,2,3,2048]{3,2,1,0:T(4,128)(4,1)S(1)} %compare_and_fusion.1), kind=kLoop, calls=%fused_computation.7.clone.clone.clone.clone | loop fusion | flops 33521664 | bytes 17006592 | tf_op jit(solution)/shard_map/while/body/eval_jaxpr/gohjr,gohjp->gohrp/dot_general | solution.py:73
  31.0 27.8 %fusion.39 = bf16[4,2,3,341,512]{4,3,2,1,0:T(8,128)(2,1)S(1)} fusion(s32[4,2,3,2048]{3,2,1,0:T(4,128)S(1)} %bitcast.280, pred[4,2,3,2048,341]{3,4,2,1,0:T(8,128)(4,1)S(1)} %fusion.251), kind=kOutput, calls=%fused_computation.42 | convolution fusion | flops 17192448000 | bytes 25337856 | tf_op jit(solution)/shard_map/while/body/eval_jaxpr/gohjr,gohjp->gohrp/dot_general | solution.py:73
  58.7 14.1 %copy.256 = bf16[4,2,3,341,512]{4,0,3,2,1:T(4,128)(2,1)S(1)} copy(bf16[4,2,3,341,512]{4,3,2,1,0:T(8,128)(2,1)S(1)} %fusion.39) | data formatting | bytes 16760832
  86.7 11.6 %fusion.249 = pred[4,2,3,2048,341]{3,4,2,1,0:T(8,128)(4,1)S(1)} fusion(s32[4,2,3,2048]{3,2,1,0:T(4,128)S(1)} %fusion.75, pred[4,2,3,2048]{3,2,1,0:T(4,128)(4,1)S(1)} %compare_and_fusion), kind=kLoop, calls=%fused_computation.8.clone.clone.clone.clone.2 | loop fusion | flops 33521664 | bytes 17006592 | tf_op jit(solution)/shard_map/while/body/eval_jaxpr/gohjr,gohjp->gohrp/dot_general | solution.py:73
  98.3 28.7 %fusion.36 = bf16[4,2,3,341,512]{4,3,2,1,0:T(8,128)(2,1)} fusion(s32[4,2,3,2048]{3,2,1,0:T(4,128)S(1)} %bitcast.281, pred[4,2,3,2048,341]{3,4,2,1,0:T(8,128)(4,1)S(1)} %fusion.249), kind=kOutput, calls=%fused_computation.41 | convolution fusion | flops 17192448000 | bytes 25337856 | tf_op jit(solution)/shard_map/while/body/eval_jaxpr/gohjr,gohjp->gohrp/dot_general | solution.py:73
  168.4 14.0 %fusion.160 = bf16[3,8,16,8,128]{4,3,2,1,0:T(8,128)(2,1)} fusion(bf16[3,2728,64]{1,2,0:T(8,128)(2,1)} %reshape.355, s32[3,2048]{1,0:T(4,128)S(1)} %convert_add_fusion.3), kind=kOutput, calls=%fused_computation.166 | convolution fusion | flops 2162540544 | bytes 1858560 | tf_op jit(solution)/shard_map/hjc,hcx->hjx/dot_general | solution.py:127
  182.4 24.8 %all-to-all-done.1 = bf16[8,3,341,128]{3,2,1,0:T(8,128)(2,1)S(1)} async-done(((bf16[8,3,341,128]{3,2,1,0:T(8,128)(2,1)}), bf16[8,3,341,128]{3,2,1,0:T(8,128)(2,1)S(1)}, u32[]{:S(2)}, u32[]{:S(2)}) %all-to-all-start.1) | async-done | bytes 2095136 | tf_op jit(solution)/shard_map/all_to_all | solution.py:186
  211.4 18.8 %fusion.63 = bf16[3,2048,128]{2,1,0:T(8,128)(2,1)S(1)} fusion(bf16[3,2728,128]{2,1,0:T(8,128)(2,1)S(1)} %reshape.358, s32[3,2048]{1,0:T(4,128)S(1)} %convert_add_fusion.2), kind=kOutput, calls=%fused_computation.86 | convolution fusion | flops 4308320256 | bytes 3692544 | tf_op jit(solution)/shard_map/hjc,hcx->hjx/dot_general | solution.py:127
  234.5 13.6 %fusion.57 = bf16[3,2728,64]{1,2,0:T(8,128)(2,1)S(1)} fusion(s32[3,2048]{1,0:T(4,128)S(1)} %convert_add_fusion.3, bf16[3,16,8,8,128]{4,3,2,1,0:T(8,128)(2,1)S(1)} %fusion.148), kind=kOutput, calls=%fused_computation.73 | convolution fusion | flops 2162671104 | bytes 1858560 | tf_op jit(solution)/shard_map/hjc,hjx->hcx/dot_general | solution.py:115
  249.9 32.9 %all_to_all.50 = bf16[8,3,341,64]{2,3,1,0:T(8,128)(2,1)S(1)} all-to-all(bf16[8,3,341,64]{2,3,1,0:T(8,128)(2,1)S(1)} %bitcast.262), channel_id=1, replica_groups=mesh['seq'=8,'head'=4] {'seq'}, dimensions={0} | all-to-all | bytes 2095104 | tf_op jit(solution)/shard_map/all_to_all | solution.py:212
  294.3 117.6 %all-reduce.3.cloned.1.call-done = f32[4,512,768]{2,1,0:T(8,128)} async-done(((f32[4,512,768]{2,1,0:T(8,128)}), f32[4,512,768]{2,1,0:T(8,128)}) %all-reduce.3.cloned.1.call-update) | async-done | bytes 6291472 | tf_op jit(solution)/shard_map/psum | solution.py:224
  425.4 18.5 %multiply_convert_fusion = (bf16[2048,768]{1,0:T(8,128)(2,1)S(1)}, f32[2048,768]{1,0:T(8,128)}, f32[2048,768]{1,0:T(8,128)}) fusion(f32[768]{0:T(1024)S(1)} %convert_element_type.271, bf16[2048,768]{1,0:T(8,128)(2,1)S(1)} %bitcast.273, bf16[768,768]{1,0:T(8,128)(2,1)S(1)} %copy-done), kind=kOutput, calls=%fused_computation.46 | convolution fusion | flops 2519728128 | bytes 20057088 | tf_op jit(solution)/shard_map/dot_general | solution.py:233
  449.9 56.9 %reduce-scatter.4.cloned.1.call-done = f32[4,128,768]{2,1,0:T(8,128)} async-done(((f32[4,512,768]{2,1,0:T(8,128)}), f32[4,128,768]{2,1,0:T(8,128)}) %reduce-scatter.4.cloned.1.call-update) | async-done | bytes 1572880 | tf_op jit(solution)/shard_map/reduce_scatter | solution.py:243
  513.1 28.4 %all-gather.3.cloned.1.call-done = bf16[4,512,768]{2,1,0:T(8,128)(2,1)} async-done(((bf16[4,128,768]{2,1,0:T(8,128)(2,1)}), bf16[4,512,768]{2,1,0:T(8,128)(2,1)}) %all-gather.3.cloned.1.call-update) | async-done | bytes 3145744 | tf_op jit(solution)/shard_map/all_gather | solution.py:257
  541.5 11.1 %fusion.208 = (f32[768]{0:T(1024)}, bf16[2048,768]{1,0:T(8,128)(2,1)S(1)}) fusion(f32[2048,768]{1,0:T(8,128)} %get-tuple-element.125, f32[2048,768]{1,0:T(8,128)} %get-tuple-element.136, f32[768]{0:T(1024)S(1)} %convert_element_type.271, bf16[2048,768]{1,0:T(8,128)(2,1)} %bitcast.284, bf16[768,768]{1,0:T(8,128)(2,1)} %param.21), kind=kOutput, calls=%fused_computation.269 | convolution fusion | flops 2441084160 | bytes 20060160 | tf_op jit(solution)/shard_map/td,fd->tf/dot_general | solution.py:260
  556.7 37.9 %reduce-scatter.6.cloned.1.call-done = bf16[4,128,768]{2,1,0:T(8,128)(2,1)} async-done(((bf16[4,512,768]{2,1,0:T(8,128)(2,1)}), bf16[4,128,768]{2,1,0:T(8,128)(2,1)}) %reduce-scatter.6.cloned.1.call-update) | async-done | bytes 786448 | tf_op jit(solution)/shard_map/reduce_scatter | solution.py:268
  602.1 28.7 %all-gather.5.cloned.1.call-done = bf16[4,512,768]{2,1,0:T(8,128)(2,1)} async-done(((bf16[4,128,768]{2,1,0:T(8,128)(2,1)}), bf16[4,512,768]{2,1,0:T(8,128)(2,1)}) %all-gather.5.cloned.1.call-update) | async-done | bytes 3145744 | tf_op jit(solution)/shard_map/all_gather | solution.py:275
  640.8 34.8 %all_to_all.51 = bf16[8,3,341,64]{2,3,1,0:T(8,128)(2,1)S(1)} all-to-all(bf16[8,3,341,64]{2,3,1,0:T(8,128)(2,1)S(1)} %bitcast.263), channel_id=1, replica_groups=mesh['seq'=8,'head'=4] {'seq'}, dimensions={0} | all-to-all | bytes 2095104 | tf_op jit(solution)/shard_map/all_to_all | solution.py:280
  677.4 11.6 %fusion.159 = bf16[3,8,16,8,128]{4,3,2,1,0:T(8,128)(2,1)S(1)} fusion(bf16[3,2728,64]{1,2,0:T(8,128)(2,1)S(1)} %reshape.369, s32[3,2048]{1,0:T(4,128)S(1)} %convert_add_fusion.3), kind=kOutput, calls=%fused_computation.165 | convolution fusion | flops 2162540544 | bytes 1858560 | tf_op jit(solution)/shard_map/hjc,hcx->hjx/dot_general | solution.py:127
  707.4 13.8 %fusion.58 = bf16[3,2728,64]{1,2,0:T(8,128)(2,1)} fusion(s32[3,2048]{1,0:T(4,128)S(1)} %copy-done.33, bf16[3,16,8,8,128]{4,3,2,1,0:T(8,128)(2,1)S(1)} %copy-done.52), kind=kOutput, calls=%fused_computation.74 | convolution fusion | flops 2162671104 | bytes 1858560 | tf_op jit(solution)/shard_map/hjc,hjx->hcx/dot_general | solution.py:115
  732.2 14.0 %fusion.56 = bf16[3,2728,128]{2,1,0:T(8,128)(2,1)} fusion(bf16[3,2048,128]{2,1,0:T(8,128)(2,1)} %bitcast.275, s32[3,2048]{1,0:T(4,128)S(1)} %copy-done.31), kind=kOutput, calls=%fused_computation.72 | convolution fusion | flops 4308581376 | bytes 3692544 | tf_op jit(solution)/shard_map/hjc,hjx->hcx/dot_general | solution.py:115
  777.6 32.1 %all-to-all-done.5 = bf16[8,3,341,128]{3,2,1,0:T(8,128)(2,1)} async-done(((bf16[8,3,341,128]{3,2,1,0:T(8,128)(2,1)}), bf16[8,3,341,128]{3,2,1,0:T(8,128)(2,1)}, u32[]{:S(2)}, u32[]{:S(2)}) %all-to-all-start.5) | async-done | bytes 2095136 | tf_op jit(solution)/shard_map/all_to_all | solution.py:310
  868.2 13.7 %all-to-all-done.8 = bf16[8,96,768]{2,1,0:T(8,128)(2,1)S(1)} async-done(((bf16[8,96,768]{2,1,0:T(8,128)(2,1)}), bf16[8,96,768]{2,1,0:T(8,128)(2,1)S(1)}, u32[]{:S(2)}, u32[]{:S(2)}) %all-to-all-start.8) | async-done | bytes 1179680 | tf_op jit(solution)/shard_map/all_to_all | solution.py:25
  913.8 41.4 %all-reduce = (f32[2,768]{1,0:T(2,128)}, f32[2,768]{1,0:T(2,128)}, f32[3072]{0:T(1024)}, f32[2,768]{1,0:T(2,128)}, f32[2,768]{1,0:T(2,128)}) all-reduce(f32[2,768]{1,0:T(2,128)S(1)} %dynamic_update_slice.11, f32[2,768]{1,0:T(2,128)S(1)} %pad_maximum_fusion.1, ...), channel_id=1, replica_groups=mesh['seq'=8,'head'=4] {'seq','head'}, use_global_device_ids=true, to_apply=%region_21.22 | all-reduce | flops 9216 | bytes 73728 | tf_op jit(solution)/shard_map/psum | solution.py:341
  (277 shorter events, 293.4 us)
Async XLA Ops:
  7.2 418.2 %copy-start = (bf16[768,768]{1,0:T(8,128)(2,1)S(1)}, bf16[768,768]{1,0:T(8,128)(2,1)}, u32[]{:S(2)}) copy-start(bf16[768,768]{1,0:T(8,128)(2,1)} %param.19) | copy-start | bytes 3538948
  77.2 76.0 %all-to-all-start = ((bf16[8,3,341,64]{2,3,1,0:T(8,128)(2,1)}), bf16[8,3,341,64]{2,3,1,0:T(8,128)(2,1)}, u32[]{:S(2)}, u32[]{:S(2)}) async-start(bf16[8,3,341,64]{2,3,1,0:T(8,128)(2,1)} %bitcast.13), calls=%async_computation | async-start | bytes 2359296 | tf_op jit(solution)/shard_map/all_to_all | solution.py:185
  153.3 54.0 %all-to-all-start.1 = ((bf16[8,3,341,128]{3,2,1,0:T(8,128)(2,1)}), bf16[8,3,341,128]{3,2,1,0:T(8,128)(2,1)S(1)}, u32[]{:S(2)}, u32[]{:S(2)}) async-start(bf16[8,3,341,128]{3,2,1,0:T(8,128)(2,1)} %bitcast.24), calls=%async_computation.1 | async-start | bytes 4227072 | tf_op jit(solution)/shard_map/all_to_all | solution.py:186
  159.2 252.7 %all-reduce.3.cloned.1.call-start = ((), (), s32[]{:S(2)}) async-start(), calls=%async_computation.13 | async-start | bytes 12582912 | tf_op jit(solution)/shard_map/psum | solution.py:224
  162.3 49.1 %copy-start.30 = (s32[3,2048]{1,0:T(4,128)}, s32[3,2048]{1,0:T(4,128)S(1)}, u32[]{:S(2)}) copy-start(s32[3,2048]{1,0:T(4,128)S(1)} %convert_add_fusion.2) | copy-start | bytes 73732
  162.4 514.9 %copy-start.32 = (s32[3,2048]{1,0:T(4,128)}, s32[3,2048]{1,0:T(4,128)S(1)}, u32[]{:S(2)}) copy-start(s32[3,2048]{1,0:T(4,128)S(1)} %convert_add_fusion.3) | copy-start | bytes 73732
  211.4 18.8 %copy-start.24 = (bf16[3,8,16,8,128]{4,3,2,1,0:T(8,128)(2,1)S(1)}, bf16[3,8,16,8,128]{4,3,2,1,0:T(8,128)(2,1)}, u32[]{:S(2)}) copy-start(bf16[3,8,16,8,128]{4,3,2,1,0:T(8,128)(2,1)} %fusion.160) | copy-start | bytes 2359300
  293.5 213.2 %reduce-scatter.4.cloned.1.call-start = ((), (), s32[]{:S(2)}) async-start(), calls=%async_computation.14 | async-start | bytes 7864320 | tf_op jit(solution)/shard_map/reduce_scatter | solution.py:243
  425.4 18.5 %copy-start.22 = (bf16[4,512,768]{2,1,0:T(8,128)(2,1)}, bf16[4,512,768]{2,1,0:T(8,128)(2,1)S(1)}, u32[]{:S(2)}) copy-start(bf16[4,512,768]{2,1,0:T(8,128)(2,1)S(1)} %get-tuple-element.126) | copy-start | bytes 9437188
  425.4 18.5 %copy-start.47 = (bf16[768,768]{1,0:T(8,128)(2,1)S(1)}, bf16[768,768]{1,0:T(8,128)(2,1)}, u32[]{:S(2)}) copy-start(bf16[768,768]{1,0:T(8,128)(2,1)} %param.21) | copy-start | bytes 3538948
  448.4 93.1 %all-gather.3.cloned.1.call-start = ((), (), s32[]{:S(2)}) async-start(), calls=%async_computation.15 | async-start | bytes 3932160 | tf_op jit(solution)/shard_map/all_gather | solution.py:257
  512.8 81.7 %reduce-scatter.6.cloned.1.call-start = ((), (), s32[]{:S(2)}) async-start(), calls=%async_computation.16 | async-start | bytes 3932160 | tf_op jit(solution)/shard_map/reduce_scatter | solution.py:268
  556.6 74.1 %all-gather.5.cloned.1.call-start = ((), (), s32[]{:S(2)}) async-start(), calls=%async_computation.17 | async-start | bytes 3932160 | tf_op jit(solution)/shard_map/all_gather | solution.py:275
  677.3 11.6 %copy-start.2 = (f32[3,16,128,128]{2,3,1,0:T(8,128)S(1)}, f32[3,16,128,128]{2,3,1,0:T(8,128)}, u32[]{:S(2)}) copy-start(f32[3,16,128,128]{2,3,1,0:T(8,128)} %copy-done.1) | copy-start | bytes 9437188
  677.3 11.6 %copy-start.26 = (f32[3,16,128]{2,1,0:T(8,128)S(1)}, f32[3,16,128]{2,1,0:T(8,128)}, u32[]{:S(2)}) copy-start(f32[3,16,128]{2,1,0:T(8,128)} %copy-done.25) | copy-start | bytes 73732
  725.1 32.2 %all-to-all-start.4 = ((bf16[8,3,341,64]{2,3,1,0:T(8,128)(2,1)}), bf16[8,3,341,64]{2,3,1,0:T(8,128)(2,1)}, u32[]{:S(2)}, u32[]{:S(2)}) async-start(bf16[8,3,341,64]{2,3,1,0:T(8,128)(2,1)} %bitcast.247), calls=%async_computation.6 | async-start | bytes 2359296 | tf_op jit(solution)/shard_map/all_to_all | solution.py:309
  757.3 52.4 %all-to-all-start.5 = ((bf16[8,3,341,128]{3,2,1,0:T(8,128)(2,1)}), bf16[8,3,341,128]{3,2,1,0:T(8,128)(2,1)}, u32[]{:S(2)}, u32[]{:S(2)}) async-start(bf16[8,3,341,128]{3,2,1,0:T(8,128)(2,1)} %copy.221), calls=%async_computation.7 | async-start | bytes 4227072 | tf_op jit(solution)/shard_map/all_to_all | solution.py:310
  809.7 37.9 %all-to-all-start.9 = ((bf16[8,768,96]{1,2,0:T(8,128)(2,1)}), bf16[8,768,96]{1,2,0:T(8,128)(2,1)S(1)}, u32[]{:S(2)}, u32[]{:S(2)}) async-start(bf16[8,768,96]{1,2,0:T(8,128)(2,1)} %bitcast.276), calls=%async_computation.12 | async-start | bytes 2359296 | tf_op jit(solution)/shard_map/all_to_all | solution.py:25
  813.3 144.3 %reduce-scatter.8.cloned.1.call-start = ((), (), s32[]{:S(2)}) async-start(), calls=%async_computation.18 | async-start | bytes 3932160 | tf_op jit(solution)/shard_map/reduce_scatter | solution.py:321
  847.6 16.5 %copy-start.14 = (bf16[8,768,96]{1,2,0:T(8,128)(2,1)}, bf16[8,768,96]{1,2,0:T(8,128)(2,1)S(1)}, u32[]{:S(2)}) copy-start(bf16[8,768,96]{1,2,0:T(8,128)(2,1)S(1)} %all-to-all-done.9) | copy-start | bytes 3538948
  847.7 34.2 %all-to-all-start.8 = ((bf16[8,96,768]{2,1,0:T(8,128)(2,1)}), bf16[8,96,768]{2,1,0:T(8,128)(2,1)S(1)}, u32[]{:S(2)}, u32[]{:S(2)}) async-start(bf16[8,96,768]{2,1,0:T(8,128)(2,1)} %bitcast.277), calls=%async_computation.11 | async-start | bytes 2359296 | tf_op jit(solution)/shard_map/all_to_all | solution.py:25
  881.9 15.8 %all-to-all-start.7 = ((bf16[8,192,96]{2,1,0:T(8,128)(2,1)}), bf16[8,192,96]{2,1,0:T(8,128)(2,1)}, u32[]{:S(2)}, u32[]{:S(2)}) async-start(bf16[8,192,96]{2,1,0:T(8,128)(2,1)} %bitcast.249), calls=%async_computation.10 | async-start | bytes 786432 | tf_op jit(solution)/shard_map/all_to_all | solution.py:25
  897.6 57.6 %all-to-all-start.6 = ((bf16[8,3,96,192]{2,3,1,0:T(8,128)(2,1)}), bf16[8,3,96,192]{2,3,1,0:T(8,128)(2,1)}, u32[]{:S(2)}, u32[]{:S(2)}) async-start(bf16[8,3,96,192]{2,3,1,0:T(8,128)(2,1)} %bitcast.246), calls=%async_computation.9 | async-start | bytes 2359296 | tf_op jit(solution)/shard_map/all_to_all | solution.py:25
  905.8 51.8 %copy-start.8 = (f32[4,128,768]{2,1,0:T(8,128)S(1)}, f32[4,128,768]{2,1,0:T(8,128)}, u32[]{:S(2)}) copy-start(f32[4,128,768]{2,1,0:T(8,128)} %copy-done.7) | copy-start | bytes 4718596
  (43 other events, 197.5 us)
Sparse Core Ops, SparseCore 0:
  293.6 118.2 all-reduce.2
  448.5 58.1 reduce-scatter.3
  513.0 28.4 all-gather.2
  556.8 37.7 reduce-scatter.5
  602.2 28.4 all-gather.4
  841.2 38.1 reduce-scatter.7
where the time goes:
time: 977 us; the launch traced here: 967 us
  waiting for transfers between devices  349 us (36%)
  matrix products  273 us (28%)
  blocking collectives  109 us (11%)
  local copies, waits for them, and re-layouts  106 us (11%)
  other arithmetic  73.8 us (8%)
  starting transfers between devices  41.2 us (4%)
  between operations  15.5 us (2%)
    psum x1, waiting for transfers between devices, per_device(): attn_whole = lax.psum(attn_part, 'head')  118 us
    reduce_scatter x1, waiting for transfers between devices, per_device(): lax.psum_scatter(ffn_part, 'head', scatter_dimension=1, tiled=True)  56.9 us
    dot_general x2, matrix products, one_group(): jnp.einsum('gohjr,gohjp->gohrp', rank_hot, pos_hot, preferred_element_typ...  56.4 us
    dot_general x3, matrix products, take_rows(): jnp.einsum('hjc,hcx->hjx', hot, flat, preferred_element_type=jnp.float32)  44.4 us
    psum x1, blocking collectives, per_device(): lax.psum((bqv_full, jnp.stack([bias_attn_grad, bias_ffn_grad]), bup_full,...  41.4 us
    dot_general x3, matrix products, place_rows(): jnp.einsum('hjc,hjx->hcx', hot, row_data, preferred_element_type=jnp.floa...  41.4 us
    unnamed x113, local copies, waits for them, and re-layouts  38.9 us
    reduce_scatter x1, waiting for transfers between devices, per_device(): lax.psum_scatter(d_first_part.astype(jnp.bfloat16), 'head', scatter_dimen...  37.9 us
  transfers between devices with their start and end apart: 14, of which 10 were waited for; matrix products, arithmetic and copies ran while one was open for 20% of the time, Pallas kernels for 0%

commit v1 on v0

v1 whole, which is shorter than its diff:
```python
import functools

import jax
import jax.numpy as jnp
from jax import lax
from jax.experimental import pallas as pl
from jax.experimental.pallas import tpu as pltpu
from jax.sharding import Mesh
from jax.sharding import PartitionSpec as P

DH = 64
FF = 3072
CLUSTER = 128
LENGTH = 4096
TOK_DEV = 2048
OWN = LENGTH // TOK_DEV
EPS = 1e-06
PLANE = ("own", "hx", "hc")
HEAD = ("hx", "hc")
SEQ = ("sq", "own")
CHUNK = 512
STEPS = 3 * TOK_DEV // CHUNK
FULL_STEPS = 2 * TOK_DEV // CHUNK
GROUPS = CHUNK // CLUSTER
BF = jnp.bfloat16
F32 = jnp.float32
VMEM = 56 * 1024 * 1024


def nn(a, b):
    return lax.dot_general(a, b, (((1,), (0,)), ((), ())), preferred_element_type=F32)


def nt(a, b):
    return lax.dot_general(a, b, (((1,), (1,)), ((), ())), preferred_element_type=F32)


def tn(a, b):
    return lax.dot_general(a, b, (((0,), (0,)), ((), ())), preferred_element_type=F32)


def project_body(x_ref, w_ref, b_ref, tq_ref, tkv_ref):
    y = (nn(x_ref[...], w_ref[...]) + b_ref[...]).astype(BF)
    for t in range(2):
        for lo in range(4):
            tq_ref[t, :, lo * DH : (lo + 1) * DH] = y[
                lo * 128 : (lo + 1) * 128, t * DH : (t + 1) * DH
            ]
        for lo in range(2):
            tkv_ref[t, :, lo * 128 : (lo + 1) * 128] = y[
                lo * 256 : (lo + 1) * 256, (t + 1) * 128 : (t + 2) * 128
            ]


def project(x_all, w_sel, b_sel):
    blocks = x_all.shape[0] // 512
    width = x_all.shape[1]
    return pl.pallas_call(
        project_body,
        grid=(blocks,),
        in_specs=[
            pl.BlockSpec((512, width), lambda j: (j, 0)),
            pl.BlockSpec((width, 384), lambda j: (0, 0)),
            pl.BlockSpec((1, 384), lambda j: (0, 0)),
        ],
        out_specs=[
            pl.BlockSpec((2, 128, 256), lambda j: (0, j, 0)),
            pl.BlockSpec((2, 256, 256), lambda j: (0, j, 0)),
        ],
        out_shape=[
            jax.ShapeDtypeStruct((2, 1024, 256), BF),
            jax.ShapeDtypeStruct((2, 2048, 256), BF),
        ],
        compiler_params=pltpu.CompilerParams(vmem_limit_bytes=VMEM),
        name="project",
    )(x_all, w_sel, b_sel)


def hot_rows(col, count):
    return (lax.broadcasted_iota(jnp.int32, (col.shape[0], count), 1) == col).astype(BF)


def hot_cols(row, count):
    return (lax.broadcasted_iota(jnp.int32, (count, row.shape[1]), 0) == row).astype(BF)


def take_quarter(table, place):
    wide = nn(hot_rows(place & 1023, 1024), table)
    lane = lax.broadcasted_iota(jnp.int32, wide.shape, 1)
    wide = jnp.where((lane >> 6) == (place >> 10), wide, 0.0)
    half = wide[:, :128] + wide[:, 128:]
    return half + pltpu.roll(half, 64, 1)


def take_half(table, place):
    wide = nn(hot_rows(place & 2047, 2048), table)
    return jnp.where((place >> 11) == 1, wide[:, 128:], wide[:, :128])


def spread_quarter(twice, place):
    wide = jnp.concatenate([twice, twice], 1)
    lane = lax.broadcasted_iota(jnp.int32, wide.shape, 1)
    return jnp.where((lane >> 6) == (place >> 10), wide, 0.0).astype(BF)


def spread_half(rows, place):
    upper = (place >> 11) == 1
    return jnp.concatenate(
        [jnp.where(upper, 0.0, rows), jnp.where(upper, rows, 0.0)], 1
    ).astype(BF)


def low_lanes(shape):
    return lax.broadcasted_iota(jnp.int32, shape, 1) < DH


def attend_body(
    pq_ref, pk_ref, pqr_ref, tq_ref, tkv_ref, q_ref, kv_ref, lt_ref, ent_ref, out_ref, acc_ref
):
    step = pl.program_id(0)
    place_q = pq_ref[0]
    twice = take_quarter(tq_ref[0], place_q)
    q_all = jnp.where(low_lanes(twice.shape), twice, 0.0).astype(BF)
    kv_all = take_half(tkv_ref[0], pk_ref[0]).astype(BF)
    q_ref[0] = q_all
    kv_ref[0] = kv_all
    outs = []
    ents = []
    for c in range(GROUPS):
        rows = slice(c * CLUSTER, (c + 1) * CLUSTER)
        q = q_all[rows]
        kv = kv_all[rows]
        scores = nt(q, kv) * (DH**-0.5)
        top = jnp.max(scores, 1, keepdims=True)
        total = jnp.sum(jnp.exp(scores - top), 1, keepdims=True)
        log_total = top + jnp.log(total)
        soft = jnp.exp(scores - log_total)
        inner = jnp.sum(soft * scores, 1, keepdims=True)
        ents.append(
            jnp.broadcast_to(jnp.sum(log_total - inner, 0, keepdims=True) / CLUSTER, (1, 128))
        )
        lt_ref[0, rows, :] = log_total
        got = nn(soft.astype(BF), kv)
        outs.append(jnp.where(low_lanes(got.shape), pltpu.roll(got, 64, 1), got))
    ent_ref[0] = jnp.concatenate(ents + ents, 0)
    spread = spread_quarter(jnp.concatenate(outs, 0), place_q)
    part = nn(hot_cols(pqr_ref[0] & 1023, 1024), spread)
    first = (step == 0) | (step == FULL_STEPS)

    @pl.when(first)
    def _():
        acc_ref[...] = part

    @pl.when(jnp.logical_not(first))
    def _():
        acc_ref[...] += part

    out_ref[0] = acc_ref[...].astype(BF)


def table_of(g):
    return g // FULL_STEPS


def attend(pq_col, pk_col, pq_row, tq, tkv):
    chunk = lambda width: pl.BlockSpec((1, CHUNK, width), lambda g: (g, 0, 0))
    return pl.pallas_call(
        attend_body,
        grid=(STEPS,),
        in_specs=[
            chunk(1),
            chunk(1),
            pl.BlockSpec((1, 1, CHUNK), lambda g: (g, 0, 0)),
            pl.BlockSpec((1, 1024, 256), lambda g: (table_of(g), 0, 0)),
            pl.BlockSpec((1, 2048, 256), lambda g: (table_of(g), 0, 0)),
        ],
        out_specs=[
            chunk(128),
            chunk(128),
            chunk(1),
            pl.BlockSpec((1, 8, 128), lambda g: (g, 0, 0)),
            pl.BlockSpec((1, 1024, 256), lambda g: (table_of(g), 0, 0)),
        ],
        out_shape=[
            jax.ShapeDtypeStruct((STEPS, CHUNK, 128), BF),
            jax.ShapeDtypeStruct((STEPS, CHUNK, 128), BF),
            jax.ShapeDtypeStruct((STEPS, CHUNK, 1), F32),
            jax.ShapeDtypeStruct((STEPS, 8, 128), F32),
            jax.ShapeDtypeStruct((2, 1024, 256), BF),
        ],
        scratch_shapes=[pltpu.VMEM((1024, 256), F32)],
        compiler_params=pltpu.CompilerParams(vmem_limit_bytes=VMEM),
        name="attend",
    )(pq_col, pk_col, pq_row, tq, tkv)


def attend_back_body(
    pq_ref, pk_ref, pqr_ref, pkr_ref, td_ref, q_ref, kv_ref, lt_ref, dq_ref, dkv_ref, accq, acckv
):
    step = pl.program_id(0)
    place_q = pq_ref[0]
    twice = take_quarter(td_ref[0], place_q)
    d_all = jnp.where(low_lanes(twice.shape), 0.0, twice).astype(BF)
    gq = []
    gkv = []
    for c in range(GROUPS):
        rows = slice(c * CLUSTER, (c + 1) * CLUSTER)
        q = q_ref[0, rows, :]
        kv = kv_ref[0, rows, :]
        d = d_all[rows]
        scores = nt(q, kv) * (DH**-0.5)
        soft = jnp.exp(scores - lt_ref[0, rows, :])
        d_soft = nt(d, kv)
        d_scores = soft * (d_soft - jnp.sum(soft * d_soft, 1, keepdims=True))
        d_raw = (d_scores * (DH**-0.5)).astype(BF)
        got = nn(d_raw, kv)
        gq.append(jnp.where(low_lanes(got.shape), got, pltpu.roll(got, 64, 1)))
        gkv.append(tn(d_raw, q) + tn(soft.astype(BF), d))
    part_q = nn(
        hot_cols(pqr_ref[0] & 1023, 1024), spread_quarter(jnp.concatenate(gq, 0), place_q)
    )
    part_kv = nn(
        hot_cols(pkr_ref[0] & 2047, 2048), spread_half(jnp.concatenate(gkv, 0), pk_ref[0])
    )
    first = (step == 0) | (step == FULL_STEPS)

    @pl.when(first)
    def _():
        accq[...] = part_q
        acckv[...] = part_kv

    @pl.when(jnp.logical_not(first))
    def _():
        accq[...] += part_q
        acckv[...] += part_kv

    @pl.when((step == FULL_STEPS - 1) | (step == STEPS - 1))
    def _():
        dq_ref[0] = accq[...].astype(BF)
        dkv_ref[0] = acckv[...].astype(BF)


def attend_back(pq_col, pk_col, pq_row, pk_row, td, q_all, kv_all, log_total):
    chunk = lambda width: pl.BlockSpec((1, CHUNK, width), lambda g: (g, 0, 0))
    line = pl.BlockSpec((1, 1, CHUNK), lambda g: (g, 0, 0))
    return pl.pallas_call(
        attend_back_body,
        grid=(STEPS,),
        in_specs=[
            chunk(1),
            chunk(1),
            line,
            line,
            pl.BlockSpec((1, 1024, 256), lambda g: (table_of(g), 0, 0)),
            chunk(128),
            chunk(128),
            chunk(1),
        ],
        out_specs=[
            pl.BlockSpec((1, 1024, 256), lambda g: (table_of(g), 0, 0)),
            pl.BlockSpec((1, 2048, 256), lambda g: (table_of(g), 0, 0)),
        ],
        out_shape=[
            jax.ShapeDtypeStruct((2, 1024, 256), BF),
            jax.ShapeDtypeStruct((2, 2048, 256), BF),
        ],
        scratch_shapes=[pltpu.VMEM((1024, 256), F32), pltpu.VMEM((2048, 256), F32)],
        compiler_params=pltpu.CompilerParams(vmem_limit_bytes=VMEM),
        name="attend_back",
    )(pq_col, pk_col, pq_row, pk_row, td, q_all, kv_all, log_total)


def project_back_body(x_ref, dq_ref, dkv_ref, w_ref, dx_ref, grad_ref, sum_ref):
    j = pl.program_id(0)
    quarters = []
    for lo in range(4):
        cols = slice(lo * DH, (lo + 1) * DH)
        quarters.append(jnp.concatenate([dq_ref[0, :, cols], dq_ref[1, :, cols]], 1))
    parts = [jnp.concatenate(quarters, 0)]
    for t in range(2):
        parts.append(jnp.concatenate([dkv_ref[t, :, :128], dkv_ref[t, :, 128:]], 0))
    rows = jnp.concatenate(parts, 1)
    dx_ref[...] = nt(rows, w_ref[...]).astype(BF)
    part = tn(x_ref[...], rows)
    sums = jnp.sum(rows.astype(F32), 0, keepdims=True)

    @pl.when(j == 0)
    def _():
        grad_ref[...] = part
        sum_ref[...] = sums

    @pl.when(j > 0)
    def _():
        grad_ref[...] += part
        sum_ref[...] += sums


def project_back(x_all, dq, dkv, w_sel):
    tokens, width = x_all.shape
    return pl.pallas_call(
        project_back_body,
        grid=(tokens // 512,),
        in_specs=[
            pl.BlockSpec((512, width), lambda j: (j, 0)),
            pl.BlockSpec((2, 128, 256), lambda j: (0, j, 0)),
            pl.BlockSpec((2, 256, 256), lambda j: (0, j, 0)),
            pl.BlockSpec((width, 384), lambda j: (0, 0)),
        ],
        out_specs=[
            pl.BlockSpec((512, width), lambda j: (j, 0)),
            pl.BlockSpec((width, 384), lambda j: (0, 0)),
            pl.BlockSpec((1, 384), lambda j: (0, 0)),
        ],
        out_shape=[
            jax.ShapeDtypeStruct((tokens, width), BF),
            jax.ShapeDtypeStruct((width, 384), F32),
            jax.ShapeDtypeStruct((1, 384), F32),
        ],
        compiler_params=pltpu.CompilerParams(vmem_limit_bytes=VMEM),
        name="project_back",
    )(x_all, dq, dkv, w_sel)


def swap(x, axis, bit=1):
    size = lax.axis_size(axis)
    return lax.ppermute(x, axis, [(i, i ^ bit) for i in range(size)])


def sum_everywhere(x):
    for axis in ("hc", "hx", "own", "sq"):
        bit = 1
        while bit < lax.axis_size(axis):
            x = x + swap(x, axis, bit)
            bit *= 2
    return x


def pick(x, index):
    return lax.dynamic_index_in_dim(x, index, 0, keepdims=False)


def sum_over_head(parts):
    hx = lax.axis_index("hx")
    hc = lax.axis_index("hc")
    by_core = jnp.moveaxis(parts, 1, 0)
    kept = pick(by_core, hc).astype(F32) + swap(pick(by_core, 1 - hc), "hc").astype(F32)
    sent = swap(pick(kept, 1 - hx).astype(BF), "hx").astype(F32)
    return pick(kept, hx) + sent


def sum_over_seq(x):
    length = lax.axis_size("sq") * lax.axis_size("own")
    tiles = lax.all_to_all(
        x.reshape(length, x.shape[0] // length, x.shape[1]), SEQ, 0, 0, tiled=True
    )
    return jnp.sum(tiles.astype(F32), 0)


def layer_norm(values, gain_row, shift_row):
    row_mean = jnp.mean(values, -1, keepdims=True)
    centred = values - row_mean
    variance = jnp.mean(centred * centred, -1, keepdims=True)
    inv_std = lax.rsqrt(variance + EPS)
    normed = centred * inv_std
    return (normed * gain_row + shift_row, normed, inv_std)


def norm_back(grad_in, normed, inv_std, gain_row):
    scaled = grad_in * gain_row
    inner_term = (
        scaled
        - jnp.mean(scaled, -1, keepdims=True)
        - normed * jnp.mean(scaled * normed, -1, keepdims=True)
    )
    return inner_term * inv_std


def per_device(
    inputs,
    w_qkv,
    b_qv,
    w_out,
    out_bias,
    w_up,
    b_up,
    w_down,
    norm_gain,
    norm_shift,
    d_out,
    q_perm,
    k_perm,
    masked,
):
    seqs, block_len, width = inputs.shape
    heads = lax.axis_size("hx") * lax.axis_size("hc")
    plane = OWN * heads
    share = block_len // heads
    tokens = seqs * share
    sq = lax.axis_index("sq")
    own = lax.axis_index("own")
    head = lax.axis_index("hx") * lax.axis_size("hc") + lax.axis_index("hc")
    part = head_cols = q_perm.shape[1] * DH

    mine = lax.dynamic_slice_in_dim(inputs, head * share, share, 1)
    x_own = lax.all_to_all(mine, "sq", 0, 0, tiled=True).reshape(tokens, width)
    x_all = lax.all_gather(x_own, PLANE, axis=0, tiled=True)
    d_own = lax.all_to_all(d_out, "sq", 0, 0, tiled=True).reshape(tokens, width)

    up_all = lax.all_gather(w_up, HEAD, axis=0, tiled=False)
    down_all = lax.all_gather(w_down, HEAD, axis=0, tiled=False)
    out_all = lax.all_gather(w_out, HEAD, axis=0, tiled=True)
    bup_all = lax.all_gather(b_up, HEAD, axis=0, tiled=True).astype(F32)

    def places(perm):
        mine = pick(perm, sq)
        full = pick(mine, 2 * own).reshape(2, TOK_DEV)
        half = lax.dynamic_slice_in_dim(mine[1], own * TOK_DEV, TOK_DEV, 0)
        pos = jnp.concatenate([full, half[None]], 0)
        block = pos // block_len
        rest = pos % block_len
        device = (block % OWN) * heads + rest // share
        return device, (block // OWN) * share + rest % share

    dev_q, tok_q = places(q_perm)
    dev_k, tok_k = places(k_perm)
    place_q = (tok_q // 128) * 1024 + dev_q * 128 + tok_q % 128
    place_k = (tok_k // 256) * 2048 + dev_k * 256 + tok_k % 256
    pq_col = place_q.reshape(STEPS, CHUNK, 1)
    pk_col = place_k.reshape(STEPS, CHUNK, 1)
    pq_row = place_q.reshape(STEPS, 1, CHUNK)
    pk_row = place_k.reshape(STEPS, 1, CHUNK)

    def two_heads(x):
        full = lax.dynamic_slice_in_dim(x, own * 2 * DH, DH, x.ndim - 1)
        return full, x[..., DH : 2 * DH]

    w_full, w_half = two_heads(w_qkv)
    w_sel = jnp.concatenate(
        [w_full[0], w_half[0], w_full[1], w_full[2], w_half[1], w_half[2]], 1
    )
    b_full, b_half = two_heads(b_qv.astype(F32))
    none = jnp.zeros((DH,), F32)
    b_sel = jnp.concatenate([b_full[0], b_half[0], none, b_full[1], none, b_half[1]])[None]
    tq, tkv = project(x_all, w_sel, b_sel)
    q_all, kv_all, log_total, ent, attended = attend(pq_col, pk_col, pq_row, tq, tkv)

    got = lax.all_to_all(
        attended.reshape(2, plane, 128, 256), PLANE, 1, 1, tiled=True
    ).reshape(2, OWN, heads, 128, 4, DH)
    shared = (got[1, 0].astype(F32) + got[1, 1].astype(F32)).astype(BF)
    head_rows = jnp.stack([got[0, 0], shared, got[0, 1]], 1)
    head_rows = head_rows.transpose(3, 2, 0, 1, 4).reshape(tokens, heads * head_cols)

    bias_out = out_bias.astype(F32)
    attn = jnp.dot(head_rows, out_all, preferred_element_type=F32)
    first_out, normed_one, inv_one = layer_norm(
        x_own.astype(F32) + attn + bias_out[0], norm_gain[0], norm_shift[0]
    )
    first_low = first_out.astype(BF)
    upper = jnp.einsum("td,hdf->thf", first_low, up_all, preferred_element_type=F32)
    upper = upper + bup_all.reshape(heads, -1)
    gelu_out, gelu_back = jax.vjp(lambda val: jax.nn.gelu(val, approximate=False), upper)
    hidden = gelu_out.astype(BF)
    ffn = jnp.einsum("thf,hfd->td", hidden, down_all, preferred_element_type=F32)
    result_own, normed_two, inv_two = layer_norm(
        first_out + ffn + bias_out[1], norm_gain[1], norm_shift[1]
    )
    result = lax.all_to_all(
        result_own.astype(BF).reshape(seqs, share, width), "sq", 0, 0, tiled=True
    ).astype(F32)

    masked_row = pick(masked, sq)
    own_pos = (
        (jnp.arange(seqs, dtype=jnp.int32) * OWN + own)[:, None] * block_len
        + head * share
        + jnp.arange(share, dtype=jnp.int32)
    ).reshape(tokens)
    mask_own = jnp.any(masked_row[:, None] == own_pos[None, :], 0).astype(F32)
    seed_grad = d_own.astype(F32) * mask_own[:, None]
    gain_two = jnp.sum(seed_grad * normed_two, 0)
    shift_two = jnp.sum(seed_grad, 0)
    d_second = norm_back(seed_grad, normed_two, inv_two, norm_gain[1])
    bias_two = jnp.sum(d_second, 0)
    d_low2 = d_second.astype(BF)
    d_hidden = jnp.einsum("td,hfd->thf", d_low2, down_all, preferred_element_type=F32)
    d_upper = gelu_back(d_hidden)[0]
    grad_bup = jnp.sum(d_upper, 0).reshape(-1)
    d_upper_low = d_upper.astype(BF)
    d_first = d_second + jnp.einsum(
        "thf,hdf->td", d_upper_low, up_all, preferred_element_type=F32
    )
    gain_one = jnp.sum(d_first * normed_one, 0)
    shift_one = jnp.sum(d_first, 0)
    d_first_in = norm_back(d_first, normed_one, inv_one, norm_gain[0])
    bias_one = jnp.sum(d_first_in, 0)
    d_attn = d_first_in.astype(BF)
    d_heads = jnp.einsum("td,cd->tc", d_attn, out_all, preferred_element_type=F32).astype(BF)
    d_heads = d_heads.reshape(4, 128, heads, 3, DH).transpose(3, 2, 1, 0, 4)
    d_heads = d_heads.reshape(3, heads, 128, 256)
    d_send = jnp.stack([d_heads[0], d_heads[2], d_heads[1], d_heads[1]], 0)
    td = lax.all_to_all(
        d_send.reshape(2, plane, 128, 256), PLANE, 1, 1, tiled=True
    ).reshape(2, plane * 128, 256)
    dq, dkv = attend_back(pq_col, pk_col, pq_row, pk_row, td, q_all, kv_all, log_total)
    dx, grad_sel, sum_sel = project_back(x_all, dq, dkv, w_sel)
    dx_own = lax.psum_scatter(dx, PLANE, scatter_dimension=0, tiled=True)
    d_in_own = d_first_in + dx_own.astype(F32)
    d_inputs = lax.all_to_all(
        d_in_own.astype(BF).reshape(seqs, share, width), "sq", 0, 0, tiled=True
    ).astype(F32)

    split = (lax.axis_size("hx"), lax.axis_size("hc"))
    down_part = jnp.einsum("td,thf->hdf", d_low2, hidden, preferred_element_type=F32).astype(BF)
    up_part = jnp.einsum("td,thf->hdf", first_low, d_upper_low, preferred_element_type=F32).astype(BF)
    out_part = jnp.einsum(
        "td,thc->hdc", d_attn, head_rows.reshape(tokens, heads, head_cols), preferred_element_type=F32
    ).astype(BF)
    down_sum, up_sum, out_sum = (
        sum_over_seq(sum_over_head(p.reshape(*split, *p.shape[1:])).astype(BF))
        for p in (down_part, up_part, out_part)
    )
    length = lax.axis_size("sq") * OWN
    qkv_tiles = lax.all_to_all(
        grad_sel.astype(BF).reshape(length, width // length, 384), SEQ, 0, 0, tiled=True
    ).reshape(length // OWN, OWN, width // length, 6, DH)
    qkv_own = jnp.sum(qkv_tiles.astype(F32), 0)

    def three_heads(full, half):
        return jnp.stack([qkv_own[0, :, full], qkv_own[0, :, half] + qkv_own[1, :, half], qkv_own[1, :, full]], 1)

    qkv_sum = jnp.stack([three_heads(0, 1), three_heads(2, 4), three_heads(3, 5)], 0)
    qkv_sum = qkv_sum.reshape(3, width // length, head_cols)

    small = sum_everywhere(
        jnp.concatenate([bias_one, bias_two, gain_one, gain_two, shift_one, shift_two, grad_bup])
    )
    obias_sum = small[: 2 * width].reshape(2, width)
    gain_sum = small[2 * width : 4 * width].reshape(2, width)
    shift_sum = small[4 * width : 6 * width].reshape(2, width)
    bup_sum = small[6 * width :]
    sums = sum_sel.reshape(6, DH)
    bqv = jnp.zeros((2, heads, 3, DH), F32)
    at_full = (jnp.arange(3) == 2 * own)[:, None]
    at_half = (jnp.arange(3) == 1)[:, None]
    at_head = (jnp.arange(heads) == head)[None, :, None, None]
    pair = jnp.stack(
        [jnp.where(at_full, sums[a], 0.0) + jnp.where(at_half, sums[b], 0.0) for a, b in ((0, 1), (3, 5))]
    )
    bqv = jnp.where(at_head, pair[:, None], 0.0).reshape(2, width)
    bqv_sum = sum_everywhere(bqv)

    ent_seg = ent[:, :GROUPS, 0].reshape(3, TOK_DEV // CLUSTER)
    ent_got = swap(jnp.where(own == 0, ent_seg[1], ent_seg[0]), "own")
    entropy = jnp.stack(
        [
            jnp.where(own == 0, ent_seg[0], ent_got),
            ent_seg[2],
            jnp.where(own == 0, ent_got, ent_seg[1]),
        ]
    )
    slots = lax.dynamic_slice_in_dim(pick(q_perm, sq), own * TOK_DEV, TOK_DEV, 1)
    slot_masked = jnp.any(slots[..., None] == masked_row[None, None, :], -1).astype(jnp.int32)
    occupancy = jnp.sum(slot_masked.reshape(slots.shape[0], TOK_DEV // CLUSTER, CLUSTER), -1)
    return (
        result,
        d_inputs,
        qkv_sum,
        bqv_sum,
        out_sum.T,
        obias_sum,
        up_sum,
        bup_sum,
        down_sum.T,
        gain_sum,
        shift_sum,
        entropy,
        occupancy,
    )


def solution(mesh):
    seq, head = (mesh.shape["seq"], mesh.shape["head"])
    fine = Mesh(
        mesh.devices.reshape(seq // OWN, OWN, 2, head // 2), ("sq", "own", "hx", "hc")
    )
    both = SEQ + HEAD
    placed = (
        P(None, SEQ, None),
        P(None, None, HEAD),
        P(None, HEAD),
        P(HEAD, None),
        P(),
        P(None, HEAD),
        P(HEAD),
        P(HEAD, None),
        P(),
        P(),
        P(None, both, None),
        P(None, HEAD, None),
        P(None, HEAD, None),
        P(),
    )
    return jax.shard_map(
        per_device,
        mesh=fine,
        in_specs=placed,
        out_specs=(
            P(None, both, None),
            P(None, both, None),
            P(None, SEQ, HEAD),
            P(),
            P(HEAD, SEQ),
            P(),
            P(SEQ, HEAD),
            P(),
            P(HEAD, SEQ),
            P(),
            P(),
            P(HEAD, SEQ),
            P(HEAD, SEQ),
        ),
        check_vma=False,
    )
```

time: 977 us -> 518 us (0.53)
  waiting for transfers between devices: 349 us -> 93.7 us
  matrix products: 273 us -> 43.4 us
  Pallas kernels: 0 us -> 112 us
  blocking collectives: 109 us -> 47.2 us
  local copies, waits for them, and re-layouts: 106 us -> 57.7 us
  starting transfers between devices: 41.2 us -> 55.9 us
  other arithmetic: 73.8 us -> 88 us
    dot_general x34 -> x9, matrix products: 271 us -> 43.4 us  [the longest x1 8.53 us: per_device(): jnp.einsum('td,hfd->thf', d_low2, down_all, preferred_element_type=F32)]
    psum x1 -> x0, waiting for transfers between devices: 118 us -> none  [per_device(): attn_whole = lax.psum(attn_part, 'head')]
    pallas_call x0 -> x4, Pallas kernels: none -> 112 us  [the longest x1 45.5 us: attend(): pl.pallas_call(attend_body, grid=(STEPS,), in_specs=[chunk(1), chunk(1),...]
    reduce_scatter x3 -> x1, waiting for transfers between devices: 94.7 us -> 0.01 us  [per_device(): dx_own = lax.psum_scatter(dx, PLANE, scatter_dimension=0, tiled=True)]
    ppermute x0 -> x17, waiting for transfers between devices: none -> 60.7 us  [swap(): return lax.ppermute(x, axis, [(i, i ^ bit) for i in range(size)])]
    all_gather x2 -> x4, waiting for transfers between devices: 57.1 us -> 0.05 us  [the longest x1 0.02 us: per_device(): out_all = lax.all_gather(w_out, HEAD, axis=0, tiled=True)]
    all_to_all x8 -> x9, waiting for transfers between devices: 79.8 us -> 31 us  [the longest x1 14 us: per_device(): lax.all_to_all(d_send.reshape(2, plane, 128, 256), PLANE, 1, 1, tiled=True)]
    psum x1 -> x0, blocking collectives: 41.4 us -> none  [per_device(): lax.psum((bqv_full, jnp.stack([bias_attn_grad, bias_ffn_grad]), bup_full,...]
  transfers between devices with their start and end apart: 14 -> 31, of which waited for: 10 -> 12; matrix products, arithmetic and copies ran while one was open for 20% -> 26% of each run, Pallas kernels for 0% -> 11%
where the time goes in v1:
time: 518 us; the launch traced here: 513 us
  Pallas kernels  112 us (22%)
  waiting for transfers between devices  93.7 us (18%)
  other arithmetic  88 us (17%)
  local copies, waits for them, and re-layouts  57.7 us (11%)
  starting transfers between devices  55.9 us (11%)
  blocking collectives  47.2 us (9%)
  matrix products  43.4 us (8%)
  between operations  15 us (3%)
    ppermute x17, waiting for transfers between devices, swap(): return lax.ppermute(x, axis, [(i, i ^ bit) for i in range(size)])  60.7 us
    pallas_call x1, Pallas kernels, attend(): pl.pallas_call(attend_body, grid=(STEPS,), in_specs=[chunk(1), chunk(1),...  45.5 us
    pallas_call x1, Pallas kernels, attend_back(): pl.pallas_call(attend_back_body, grid=(STEPS,), in_specs=[chunk(1), chunk...  44.4 us
    all_to_all x1, blocking collectives, per_device(): x_own = lax.all_to_all(mine, 'sq', 0, 0, tiled=True).reshape(tokens, width)  26.4 us
    all_gather x1, blocking collectives, per_device(): bup_all = lax.all_gather(b_up, HEAD, axis=0, tiled=True).astype(F32)  20.8 us
    convert_element_type x1, other arithmetic, per_device(): hidden = gelu_out.astype(BF)  15.7 us
    all_to_all x3, starting transfers between devices, sum_over_seq(): lax.all_to_all(x.reshape(length, x.shape[0] // length, x.shape[1]), SEQ,...  15.3 us
    ppermute x17, starting transfers between devices, swap(): return lax.ppermute(x, axis, [(i, i ^ bit) for i in range(size)])  14.7 us
  transfers between devices with their start and end apart: 31, of which 12 were waited for; matrix products, arithmetic and copies ran while one was open for 26% of the time, Pallas kernels for 11%

profile of v1, /device:TPU:0, one launch (start us, length us, event | category | flops | bytes accessed | tf_op | source)
XLA Modules:
  0.0 513.2 jit_solution(17547020002969485012)
XLA Ops:
  9.1 26.4 %all_to_all.50 = bf16[4,128,768]{2,1,0:T(8,128)(2,1)} all-to-all(bf16[4,128,768]{2,1,0:T(8,128)(2,1)S(1)} %constant_dynamic-slice_fusion.6), channel_id=1, replica_groups=mesh['sq'=4,'own'=2,'hx'=2,'hc'=2] {'sq'}, dimensions={0} | all-to-all | bytes 1572864 | tf_op jit(solution)/shard_map/all_to_all | solution.py:405
  46.9 12.7 %fusion.18.pk_ref = s32[12,512,1]{2,1,0:T(8,128)} fusion(s32[12,512,1]{2,1,0:T(8,128)S(1)} %concatenate.34), kind=kLoop, calls=%fused_computation.76 | loop fusion | flops 516096 | bytes 49152 | tf_op jit(solution)/shard_map/add | solution.py:427
  62.7 12.4 %fusion.10.pq_ref = s32[12,512,1]{2,1,0:T(8,128)} fusion(s32[12,512,1]{2,1,0:T(8,128)S(1)} %concatenate.33), kind=kLoop, calls=%fused_computation.68 | loop fusion | flops 516096 | bytes 49152 | tf_op jit(solution)/shard_map/add | solution.py:426
  80.7 9.4 %project.1 = (bf16[2,1024,256]{2,1,0:T(8,128)(2,1)}, bf16[2,2048,256]{2,1,0:T(8,128)(2,1)}) custom-call(bf16[4096,768]{1,0:T(8,128)(2,1)} %all-gather.8.cloned.1.call-done.x_ref, bf16[768,384]{1,0:T(8,128)(2,1)} %concatenate.29.w_ref, f32[1,384]{1,0:T(1,128)} %broadcast_in_dim.108.b_ref), custom_call_target="tpu_custom_call" | custom-call | tf_op jit(solution)/shard_map/project/pallas_call | solution.py:58
  90.2 45.5 %attend.1 = (bf16[12,512,128]{2,1,0:T(8,128)(2,1)}, bf16[12,512,128]{2,1,0:T(8,128)(2,1)}, f32[12,512,1]{2,1,0:T(8,128)}, f32[12,8,128]{2,1,0:T(8,128)}, bf16[2,1024,256]{2,1,0:T(8,128)(2,1)}) custom-call(s32[12,512,1]{2,1,0:T(8,128)} %fusion.10.pq_ref, s32[12,512,1]{2,1,0:T(8,128)} %fusion.18.pk_ref, s32[12,1,512]{2,1,0:T(1,128)} %fusion.74.pqr_ref, ...), custom_call_target="tpu_custom_call" | custom-call | tf_op jit(solution)/shard_map/attend/pallas_call | solution.py:167
  142.9 20.8 %all-gather.2 = bf16[4,1,768]{2,1,0:T(2,128)(2,1)S(1)} all-gather(bf16[1,1,768]{2,1,0:T(2,128)(2,1)S(1)} %reshape.1845), channel_id=1, replica_groups=mesh['sq'=4,'own'=2,'hx'=2,'hc'=2] {'hx','hc'}, dimensions={0}, use_global_device_ids=true | all-gather | bytes 7680 | tf_op jit(solution)/shard_map/all_gather | solution.py:412
  169.3 6.5 %fusion.49 = (u8[512,768]{1,0:T(8,128)(4,1)S(1)}, u8[512,768]{1,0:T(8,128)(4,1)S(1)}, f32[512,4,768]{2,0,1:T(8,128)S(1)}) fusion(f32[4,768]{1,0:T(4,128)S(1)} %bitcast.232, bf16[4,768,768]{2,1,0:T(8,128)(2,1)} %bitcast.238, f32[512,768]{1,0:T(8,128)S(1)} %get-tuple-element.166, f32[768]{0:T(1024)S(1)} %get-tuple-element.118, ...), kind=kOutput, calls=%fused_computation.143 | convolution fusion | flops 2439118848 | bytes 13391872 | tf_op jit(solution)/shard_map/td,hdf->thf/dot_general | solution.py:460
  178.5 15.7 %multiply_convert_fusion = (bf16[512,4,768]{2,0,1:T(8,128)(2,1)}, f32[512,4,768]{2,0,1:T(8,128)}) fusion(f32[512,4,768]{2,0,1:T(8,128)S(1)} %get-tuple-element.167, f32[4,768]{1,0:T(4,128)S(1)} %bitcast.233, u8[512,768]{1,0:T(8,128)(4,1)S(1)} %get-tuple-element.103, u8[512,768]{1,0:T(8,128)(4,1)S(1)} %get-tuple-element.102), kind=kLoop, calls=%fused_computation.9 | loop fusion | flops 111673344 | bytes 16527360 | tf_op jit(solution)/shard_map/convert_element_type | solution.py:463
  194.2 6.8 %fusion.93 = (f32[512]{0:T(512)S(1)}, f32[512,768]{1,0:T(8,128)S(1)}) fusion(f32[768]{0:T(1024)S(1)} %get-tuple-element.119, bf16[512,4,768]{2,0,1:T(8,128)(2,1)} %get-tuple-element.125, bf16[4,768,768]{2,1,0:T(8,128)(2,1)} %bitcast.240, f32[768]{0:T(1024)S(1)} %get-tuple-element.118, f32[768]{0:T(1024)S(1)} %get-tuple-element.179, ...), kind=kOutput, calls=%fused_computation.314 | convolution fusion | flops 2418671104 | bytes 11025408 | tf_op jit(solution)/shard_map/thf,hfd->td/dot_general | solution.py:464
  206.1 8.5 %fusion.94 = (f32[4,768]{1,0:T(4,128)S(1)}, bf16[512,4,768]{2,0,1:T(8,128)(2,1)}) fusion(f32[512,4,768]{2,0,1:T(8,128)S(1)} %copy-done.5, bf16[4,768,768]{2,1,0:T(8,128)(2,1)} %bitcast.241, f32[512,768]{1,0:T(8,128)S(1)} %get-tuple-element.122, f32[512,4,768]{2,0,1:T(8,128)S(1)} %copy-done.4, f32[4,768]{1,0:T(4,128)S(1)} %bitcast.234), kind=kOutput, calls=%fused_computation.315 | convolution fusion | flops 2441475072 | bytes 22044672 | tf_op jit(solution)/shard_map/td,hfd->thf/dot_general | solution.py:485
  214.7 6.4 %multiply_reduce_fusion.1 = (f32[768]{0:T(1024)S(1)}, f32[512]{0:T(512)S(1)}, f32[512]{0:T(512)S(1)}, f32[768]{0:T(1024)S(1)}, f32[512,768]{1,0:T(8,128)S(1)}) fusion(f32[512,768]{1,0:T(8,128)S(1)} %get-tuple-element.166, f32[512]{0:T(512)S(1)} %add_rsqrt_fusion.1, f32[512]{0:T(512)S(1)} %broadcast_multiply_fusion.4, f32[768]{0:T(1024)S(1)} %get-tuple-element.179, ...), kind=kOutput, calls=%fused_computation.127 | convolution fusion | flops 2419848704 | bytes 12600320 | tf_op jit(solution)/shard_map/thf,hdf->td/dot_general | solution.py:489
  239.7 14.0 %all-to-all-done.4 = bf16[2,8,128,256]{3,2,0,1:T(8,128)(2,1)} async-done(((bf16[2,8,128,256]{3,2,0,1:T(8,128)(2,1)}), bf16[2,8,128,256]{3,2,0,1:T(8,128)(2,1)}, u32[]{:S(2)}, u32[]{:S(2)}) %all-to-all-start.4) | async-done | bytes 1048608 | tf_op jit(solution)/shard_map/all_to_all | solution.py:501
  256.0 44.4 %attend_back.1 = (bf16[2,1024,256]{2,1,0:T(8,128)(2,1)}, bf16[2,2048,256]{2,1,0:T(8,128)(2,1)}) custom-call(s32[12,512,1]{2,1,0:T(8,128)} %fusion.10.pq_ref, s32[12,512,1]{2,1,0:T(8,128)} %fusion.18.pk_ref, s32[12,1,512]{2,1,0:T(1,128)} %fusion.74.pqr_ref, s32[12,1,512]{2,1,0:T(1,128)} %fusion.76.pkr_ref, bf16[2,1024,256]{2,1,0:T(8,128)(2,1)} %bitcast.210, ...), custom_call_target="tpu_custom_call" | custom-call | tf_op jit(solution)/shard_map/attend_back/pallas_call | solution.py:246
  300.3 13.1 %project_back.1 = (bf16[4096,768]{1,0:T(8,128)(2,1)}, f32[768,384]{1,0:T(8,128)}, f32[1,384]{1,0:T(1,128)}) custom-call(bf16[4096,768]{1,0:T(8,128)(2,1)} %all-gather.8.cloned.1.call-done.x_ref, bf16[2,1024,256]{2,1,0:T(8,128)(2,1)} %get-tuple-element.31.dq_ref, bf16[2,2048,256]{2,1,0:T(8,128)(2,1)} %get-tuple-element.32.dkv_ref, ...), custom_call_target="tpu_custom_call" | custom-call | tf_op jit(solution)/shard_map/project_back/pallas_call | solution.py:300
  325.2 5.7 %all-to-all-start.2 = ((bf16[4,128,768]{2,1,0:T(8,128)(2,1)}), bf16[4,128,768]{2,1,0:T(8,128)(2,1)}, u32[]{:S(2)}, u32[]{:S(2)}) async-start(bf16[4,128,768]{2,1,0:T(8,128)(2,1)} %bitcast.211), calls=%async_computation.2 | async-start | bytes 1572864 | tf_op jit(solution)/shard_map/all_to_all | solution.py:468
  332.8 5.0 convolution_convert_fusion
  345.2 5.1 convert_add_fusion.1
  361.2 5.4 %all-to-all-done.7 = bf16[8,96,192]{1,2,0:T(8,128)(2,1)S(1)} async-done(((bf16[8,96,192]{1,2,0:T(8,128)(2,1)}), bf16[8,96,192]{1,2,0:T(8,128)(2,1)S(1)}, u32[]{:S(2)}, u32[]{:S(2)}) %all-to-all-start.7) | async-done | bytes 294944 | tf_op jit(solution)/shard_map/all_to_all | solution.py:353
  375.0 19.1 %collective-permute-done.13 = bf16[768,768]{1,0:T(8,128)(2,1)} collective-permute-done((bf16[768,768]{1,0:T(8,128)(2,1)}, bf16[768,768]{1,0:T(8,128)(2,1)}, u32[]{:S(2)}, u32[]{:S(2)}) %collective-permute-start.13) | collective-permute-done | bytes 1179680 | tf_op jit(solution)/shard_map/ppermute | solution.py:326
  398.3 5.5 %all-to-all-start.8 = ((bf16[8,96,768]{2,1,0:T(8,128)(2,1)}), bf16[8,96,768]{2,1,0:T(8,128)(2,1)S(1)}, u32[]{:S(2)}, u32[]{:S(2)}) async-start(bf16[8,96,768]{2,1,0:T(8,128)(2,1)} %bitcast.73), calls=%async_computation.9 | async-start | bytes 2359296 | tf_op jit(solution)/shard_map/all_to_all | solution.py:353
  413.5 22.4 %collective-permute-done.15 = bf16[768,768]{1,0:T(8,128)(2,1)} collective-permute-done((bf16[768,768]{1,0:T(8,128)(2,1)}, bf16[768,768]{1,0:T(8,128)(2,1)}, u32[]{:S(2)}, u32[]{:S(2)}) %collective-permute-start.15) | collective-permute-done | bytes 1179680 | tf_op jit(solution)/shard_map/ppermute | solution.py:326
  439.2 5.7 %all-to-all-start.9 = ((bf16[8,96,768]{2,1,0:T(8,128)(2,1)}), bf16[8,96,768]{2,1,0:T(8,128)(2,1)}, u32[]{:S(2)}, u32[]{:S(2)}) async-start(bf16[8,96,768]{2,1,0:T(8,128)(2,1)} %bitcast.82), calls=%async_computation.10 | async-start | bytes 2359296 | tf_op jit(solution)/shard_map/all_to_all | solution.py:353
  456.3 5.6 %collective-permute-done.10 = f32[7680]{0:T(1024)S(1)} collective-permute-done((f32[7680]{0:T(1024)S(1)}, f32[7680]{0:T(1024)S(1)}, u32[]{:S(2)}, u32[]{:S(2)}) %collective-permute-start.10) | collective-permute-done | bytes 30752 | tf_op jit(solution)/shard_map/ppermute | solution.py:326
  493.9 10.1 %all-to-all-done.5 = bf16[4,128,768]{2,1,0:T(8,128)(2,1)} async-done(((bf16[4,128,768]{2,1,0:T(8,128)(2,1)}), bf16[4,128,768]{2,1,0:T(8,128)(2,1)}, u32[]{:S(2)}, u32[]{:S(2)}) %all-to-all-start.5) | async-done | bytes 786464 | tf_op jit(solution)/shard_map/all_to_all | solution.py:508
  (250 shorter events, 166.1 us)
Async XLA Ops:
  7.2 73.6 %all-gather.8.cloned.1.call-start = ((), (), s32[]{:S(2)}) async-start(), calls=%async_computation.11 | async-start | bytes 7077888 | tf_op jit(solution)/shard_map/all_gather | solution.py:406
  35.5 130.7 %all-gather.10.cloned.1.call-start = ((), (), s32[]{:S(2)}) async-start(), calls=%async_computation.12 | async-start | bytes 1474560 | tf_op jit(solution)/shard_map/all_gather | solution.py:411
  36.3 133.0 %all-gather.12.cloned.1.call-start = ((), (), s32[]{:S(2)}) async-start(), calls=%async_computation.14 | async-start | bytes 5898240 | tf_op jit(solution)/shard_map/all_gather | solution.py:409
  37.0 100.9 %all-to-all-start.3 = ((bf16[4,128,768]{2,1,0:T(8,128)(2,1)}), bf16[4,128,768]{2,1,0:T(8,128)(2,1)}, u32[]{:S(2)}, u32[]{:S(2)}) async-start(bf16[4,128,768]{2,1,0:T(8,128)(2,1)} %param.24), calls=%async_computation.3 | async-start | bytes 1572864 | tf_op jit(solution)/shard_map/all_to_all | solution.py:407
  41.2 153.0 %all-gather.14.cloned.1.call-start = ((), (), s32[]{:S(2)}) async-start(), calls=%async_computation.15 | async-start | bytes 5898240 | tf_op jit(solution)/shard_map/all_gather | solution.py:410
  138.0 27.3 %all-to-all-start.1 = ((bf16[2,8,128,256]{2,3,0,1:T(8,128)(2,1)}), bf16[2,8,128,256]{2,3,0,1:T(8,128)(2,1)S(1)}, u32[]{:S(2)}, u32[]{:S(2)}) async-start(bf16[2,8,128,256]{2,3,0,1:T(8,128)(2,1)} %copy.154), calls=%async_computation.1 | async-start | bytes 2097152 | tf_op jit(solution)/shard_map/all_to_all | solution.py:447
  234.0 19.6 %all-to-all-start.4 = ((bf16[2,8,128,256]{3,2,0,1:T(8,128)(2,1)}), bf16[2,8,128,256]{3,2,0,1:T(8,128)(2,1)}, u32[]{:S(2)}, u32[]{:S(2)}) async-start(bf16[2,8,128,256]{3,2,0,1:T(8,128)(2,1)} %copy.161), calls=%async_computation.4 | async-start | bytes 2097152 | tf_op jit(solution)/shard_map/all_to_all | solution.py:501
  238.3 243.6 %reduce-scatter.2.cloned.1.call-start = ((), (), s32[]{:S(2)}) async-start(), calls=%async_computation.13 | async-start | bytes 7077888 | tf_op jit(solution)/shard_map/reduce_scatter | solution.py:506
  322.4 22.7 %collective-permute-start.12 = (bf16[2,768,768]{2,1,0:T(8,128)(2,1)}, bf16[2,768,768]{2,1,0:T(8,128)(2,1)}, u32[]{:S(2)}, u32[]{:S(2)}) collective-permute-start(bf16[2,768,768]{2,1,0:T(8,128)(2,1)} %dynamic-slice_bitcast_fusion.1), channel_id=1, source_target_pairs={{0,1},{1,0},{2,3},{3,2},{4,5},{5,4},{6,7},{7,6},{8,9},{9,8},{10,11... | collective-permute-start | bytes 7077896 | tf_op jit(solution)/shard_map/ppermute | solution.py:326
  325.2 26.6 %all-to-all-start.2 = ((bf16[4,128,768]{2,1,0:T(8,128)(2,1)}), bf16[4,128,768]{2,1,0:T(8,128)(2,1)}, u32[]{:S(2)}, u32[]{:S(2)}) async-start(bf16[4,128,768]{2,1,0:T(8,128)(2,1)} %bitcast.211), calls=%async_computation.2 | async-start | bytes 1572864 | tf_op jit(solution)/shard_map/all_to_all | solution.py:468
  332.2 11.7 %collective-permute-start.6 = (bf16[768,192]{0,1:T(8,128)(2,1)S(1)}, bf16[768,192]{0,1:T(8,128)(2,1)S(1)}, u32[]{:S(2)}, u32[]{:S(2)}) collective-permute-start(bf16[768,192]{0,1:T(8,128)(2,1)S(1)} %fusion.68), channel_id=1, source_target_pairs={{0,2},{2,0},{1,3},{3,1},{4,6},{6,4},{5,7},{7,5},{8,10},{10,8},{9,1... | collective-permute-start | bytes 884744 | tf_op jit(solution)/shard_map/ppermute | solution.py:326
  341.6 62.2 %collective-permute-start.14 = (bf16[2,768,768]{2,1,0:T(8,128)(2,1)}, bf16[2,768,768]{2,1,0:T(8,128)(2,1)}, u32[]{:S(2)}, u32[]{:S(2)}) collective-permute-start(bf16[2,768,768]{2,1,0:T(8,128)(2,1)} %dynamic-slice_bitcast_fusion), channel_id=1, source_target_pairs={{0,1},{1,0},{2,3},{3,2},{4,5},{5,4},{6,7},{7,6},{8,9},{9,8},{10,11... | collective-permute-start | bytes 7077896 | tf_op jit(solution)/shard_map/ppermute | solution.py:326
  351.8 14.9 %all-to-all-start.7 = ((bf16[8,96,192]{1,2,0:T(8,128)(2,1)}), bf16[8,96,192]{1,2,0:T(8,128)(2,1)S(1)}, u32[]{:S(2)}, u32[]{:S(2)}) async-start(bf16[8,96,192]{1,2,0:T(8,128)(2,1)} %copy.166), calls=%async_computation.8 | async-start | bytes 786432 | tf_op jit(solution)/shard_map/all_to_all | solution.py:353
  358.6 35.5 %collective-permute-start.13 = (bf16[768,768]{1,0:T(8,128)(2,1)}, bf16[768,768]{1,0:T(8,128)(2,1)}, u32[]{:S(2)}, u32[]{:S(2)}) collective-permute-start(bf16[768,768]{1,0:T(8,128)(2,1)} %fusion.55), channel_id=1, source_target_pairs={{0,2},{2,0},{1,3},{3,1},{4,6},{6,4},{5,7},{7,5},{8,10},{10,8},{9,1... | collective-permute-start | bytes 3538952 | tf_op jit(solution)/shard_map/ppermute | solution.py:326
  366.6 30.8 %all-to-all-start.6 = ((bf16[8,96,384]{2,1,0:T(8,128)(2,1)}), bf16[8,96,384]{2,1,0:T(8,128)(2,1)S(1)}, u32[]{:S(2)}, u32[]{:S(2)}) async-start(bf16[8,96,384]{2,1,0:T(8,128)(2,1)} %bitcast.38), calls=%async_computation.7 | async-start | bytes 1179648 | tf_op jit(solution)/shard_map/all_to_all | solution.py:523
  398.3 40.9 %all-to-all-start.8 = ((bf16[8,96,768]{2,1,0:T(8,128)(2,1)}), bf16[8,96,768]{2,1,0:T(8,128)(2,1)S(1)}, u32[]{:S(2)}, u32[]{:S(2)}) async-start(bf16[8,96,768]{2,1,0:T(8,128)(2,1)} %bitcast.73), calls=%async_computation.9 | async-start | bytes 2359296 | tf_op jit(solution)/shard_map/all_to_all | solution.py:353
  410.0 25.9 %collective-permute-start.15 = (bf16[768,768]{1,0:T(8,128)(2,1)}, bf16[768,768]{1,0:T(8,128)(2,1)}, u32[]{:S(2)}, u32[]{:S(2)}) collective-permute-start(bf16[768,768]{1,0:T(8,128)(2,1)} %fusion.56), channel_id=1, source_target_pairs={{0,2},{2,0},{1,3},{3,1},{4,6},{6,4},{5,7},{7,5},{8,10},{10,8},{9,1... | collective-permute-start | bytes 3538952 | tf_op jit(solution)/shard_map/ppermute | solution.py:326
  412.0 33.4 %collective-permute-start.8 = (f32[7680]{0:T(1024)S(1)}, f32[7680]{0:T(1024)S(1)}, u32[]{:S(2)}, u32[]{:S(2)}) collective-permute-start(f32[7680]{0:T(1024)S(1)} %add.827), channel_id=1, source_target_pairs={{0,2},{2,0},{1,3},{3,1},{4,6},{6,4},{5,7},{7,5},{8,10},{10,8},{9,1... | collective-permute-start | bytes 92168 | tf_op jit(solution)/shard_map/ppermute | solution.py:326
  439.2 44.9 %all-to-all-start.9 = ((bf16[8,96,768]{2,1,0:T(8,128)(2,1)}), bf16[8,96,768]{2,1,0:T(8,128)(2,1)}, u32[]{:S(2)}, u32[]{:S(2)}) async-start(bf16[8,96,768]{2,1,0:T(8,128)(2,1)} %bitcast.82), calls=%async_computation.10 | async-start | bytes 2359296 | tf_op jit(solution)/shard_map/all_to_all | solution.py:353
  447.6 8.6 %collective-permute-start.1 = (f32[2,768]{1,0:T(2,128)S(1)}, f32[2,768]{1,0:T(2,128)S(1)}, u32[]{:S(2)}, u32[]{:S(2)}) collective-permute-start(f32[2,768]{1,0:T(2,128)S(1)} %fusion.106), channel_id=1, source_target_pairs={{0,2},{2,0},{1,3},{3,1},{4,6},{6,4},{5,7},{7,5},{8,10},{10,8},{9,1... | collective-permute-start | bytes 18440 | tf_op jit(solution)/shard_map/ppermute | solution.py:326
  452.8 9.1 %collective-permute-start.10 = (f32[7680]{0:T(1024)S(1)}, f32[7680]{0:T(1024)S(1)}, u32[]{:S(2)}, u32[]{:S(2)}) collective-permute-start(f32[7680]{0:T(1024)S(1)} %add.829), channel_id=1, source_target_pairs={{0,8},{8,0},{16,24},{24,16},{1,9},{9,1},{17,25},{25,17},{2,10},{10... | collective-permute-start | bytes 92168 | tf_op jit(solution)/shard_map/ppermute | solution.py:326
  456.2 9.8 %collective-permute-start.2 = (f32[2,768]{1,0:T(2,128)S(1)}, f32[2,768]{1,0:T(2,128)S(1)}, u32[]{:S(2)}, u32[]{:S(2)}) collective-permute-start(f32[2,768]{1,0:T(2,128)S(1)} %add.817), channel_id=1, source_target_pairs={{0,4},{4,0},{1,5},{5,1},{2,6},{6,2},{3,7},{7,3},{8,12},{12,8},{9,1... | collective-permute-start | bytes 18440 | tf_op jit(solution)/shard_map/ppermute | solution.py:326
  461.9 9.3 %collective-permute-start.11 = (f32[7680]{0:T(1024)S(1)}, f32[7680]{0:T(1024)S(1)}, u32[]{:S(2)}, u32[]{:S(2)}) collective-permute-start(f32[7680]{0:T(1024)S(1)} %add.830), channel_id=1, source_target_pairs={{0,16},{8,24},{16,0},{24,8},{1,17},{9,25},{17,1},{25,9},{2,18},{10... | collective-permute-start | bytes 92168 | tf_op jit(solution)/shard_map/ppermute | solution.py:326
  484.1 19.9 %all-to-all-start.5 = ((bf16[4,128,768]{2,1,0:T(8,128)(2,1)}), bf16[4,128,768]{2,1,0:T(8,128)(2,1)}, u32[]{:S(2)}, u32[]{:S(2)}) async-start(bf16[4,128,768]{2,1,0:T(8,128)(2,1)} %bitcast.37), calls=%async_computation.6 | async-start | bytes 1572864 | tf_op jit(solution)/shard_map/all_to_all | solution.py:508
  (30 other events, 263.4 us)
Sparse Core Ops, SparseCore 0:
  35.6 44.4 all-gather.7
  81.7 17.4 all-gather.9
  100.8 37.4 all-gather.11
  139.6 43.4 all-gather.13
  313.6 71.8 reduce-scatter.1
